TPU v7x, 128 devices: a whole 4x4x4 slice. The times are simulated.
128 devices in a mesh: section: 8 (over z_hi, x), seq: 16 (over z_lo, y, core).
Axes of the slice: x: 4, y: 4, z: 4 (z_hi: 2, z_lo: 2; z = z_hi * 2 + z_lo), core: 2. Of those that a mesh axis runs over, the one named last changes fastest.
Arguments:
- grad_out: bfloat16 [8, 2048, 8192], P('section', 'seq'), may hold values from -7.5 to 7.5
- queries: bfloat16 [8, 2048, 8192], P('section', 'seq'), may hold values from -2.5 to 2.5
- mem_out: bfloat16 [8, 2048, 8192], P('section', 'seq'), may hold values from -6 to 6
- row_total: bfloat16 [8, 2048, 64], P('section', 'seq'), may hold values from 8192 to 32768
- gate_logit: float32 [8, 64], P('section'), may hold values from -2 to 2
- mem_keys: bfloat16 [8, 16384, 1024], P('section', 'seq'), may hold values from -3.5 to 3.5
- mem_values: bfloat16 [8, 16384, 1024], P('section', 'seq'), may hold values from -7.5 to 7.5
- retrieved: int32 [8, 8, 16, 32], P('section'), may hold values from 0 to 127, all different within a row
Outputs:
- onward: bfloat16 [8, 2048, 8192], P('section', 'seq')
Inputs may be any that keep to these rules, and one draw needn't show every extreme that they name: `retrieved`: 32 different memory blocks for each section, key head and query block; every memory block is named somewhere, some far more often than others.
All inputs are finite; a program needn't handle non-finite values.
Results may differ from a plain program's by a relative error of at most 0.0054.
Values may be sent and summed in bfloat16 or wider, within the bound.
A program may use at most 128 MiB of HBM per device.

v0:
```python
import jax
import jax.numpy as jnp
from jax import lax
from jax.sharding import PartitionSpec as P

BLOCK = 128


def passed_along(value, axis, steps):
    count = lax.axis_size(axis)
    pairs = [(source, (source + steps) % count) for source in range(count)]
    return lax.ppermute(value, axis, pairs)


def shards(grad_out, queries, mem_out, row_total, gate_logit, mem_keys, mem_values, retrieved):
    seq_count = lax.axis_size("seq")
    position = lax.axis_index("seq")
    tok_dev = grad_out.shape[1]
    full_width = grad_out.shape[2]
    head_count = gate_logit.shape[1]
    head_dim = full_width // head_count
    kv_heads = mem_keys.shape[2] // head_dim
    copies = seq_count // kv_heads
    local_heads = head_count // seq_count
    group_size = head_count // kv_heads
    mem_dev = mem_keys.shape[1]
    score_scale = head_dim ** (-0.5)
    gate_values = jax.nn.sigmoid(gate_logit[0])
    grad_three = (
        gate_values[None, :, None]
        * grad_out[0].reshape(tok_dev, head_count, head_dim).astype(jnp.float32)
    ).astype(jnp.bfloat16)
    token_delta = jnp.sum(
        grad_three.astype(jnp.float32)
        * mem_out[0].reshape(tok_dev, head_count, head_dim).astype(jnp.float32),
        axis=-1,
    )
    grad_mem = grad_three.reshape(tok_dev, full_width)
    head_grad, head_query = (
        lax.all_to_all(grad_mem, "seq", split_axis=1, concat_axis=0, tiled=True),
        lax.all_to_all(queries[0], "seq", split_axis=1, concat_axis=0, tiled=True),
    )
    row_delta, head_sum = (
        lax.all_to_all(token_delta, "seq", split_axis=1, concat_axis=0, tiled=True),
        lax.all_to_all(
            row_total[0].astype(jnp.float32), "seq", split_axis=1, concat_axis=0, tiled=True
        ),
    )
    tokens = head_grad.shape[0]
    kv_index = position * local_heads // group_size
    chosen = lax.dynamic_index_in_dim(retrieved[0], kv_index, 0, keepdims=False)
    keys_three = mem_keys[0].reshape(mem_dev, kv_heads, head_dim)
    values_three = mem_values[0].reshape(mem_dev, kv_heads, head_dim)
    keys_repeat = jnp.repeat(keys_three, copies, axis=1)
    values_repeat = jnp.repeat(values_three, copies, axis=1)
    head_keys, head_values = (
        lax.all_to_all(keys_repeat, "seq", split_axis=1, concat_axis=0, tiled=True),
        lax.all_to_all(values_repeat, "seq", split_axis=1, concat_axis=0, tiled=True),
    )
    key_blocks = head_keys.reshape(-1, BLOCK, head_dim)
    value_blocks = head_values.reshape(-1, BLOCK, head_dim)

    def one_block(pieces):
        query_tile, grad_tile, delta_tile, sum_tile, picks = pieces
        tile_keys = key_blocks[picks].reshape(-1, head_dim)
        tile_values = value_blocks[picks].reshape(-1, head_dim)
        scores = (
            jnp.einsum("qhd,kd->qhk", query_tile, tile_keys, preferred_element_type=jnp.float32)
            * score_scale
        )
        probs = jnp.exp(scores - jnp.log(sum_tile)[:, :, None])
        grad_probs = jnp.einsum(
            "qhd,kd->qhk", grad_tile, tile_values, preferred_element_type=jnp.float32
        )
        grad_scores = (probs * (grad_probs - delta_tile[:, :, None]) * score_scale).astype(
            jnp.bfloat16
        )
        result = jnp.einsum(
            "qhk,kd->qhd", grad_scores, tile_keys, preferred_element_type=jnp.float32
        )
        return result.astype(jnp.bfloat16)

    query_blocks = tokens // BLOCK
    blocks_in = (
        head_query.reshape(query_blocks, BLOCK, local_heads, head_dim),
        head_grad.reshape(query_blocks, BLOCK, local_heads, head_dim),
        row_delta.reshape(query_blocks, BLOCK, local_heads),
        head_sum.reshape(query_blocks, BLOCK, local_heads),
        chosen,
    )
    grads = lax.map(one_block, blocks_in).reshape(tokens, local_heads * head_dim)
    returned = lax.all_to_all(grads, "seq", split_axis=0, concat_axis=1, tiled=True)
    delivered = passed_along(returned, "section", -1)
    return delivered[None]


def solution(mesh):
    return jax.shard_map(
        shards,
        mesh=mesh,
        in_specs=(
            P("section", "seq", None),
            P("section", "seq", None),
            P("section", "seq", None),
            P("section", "seq", None),
            P("section", None),
            P("section", "seq", None),
            P("section", "seq", None),
            P("section", None, None, None),
        ),
        out_specs=P("section", "seq", None),
        check_vma=False,
    )
```

profile of v0, /device:TPU:13, one launch (start us, length us, event | category | flops | bytes accessed | tf_op | source)
XLA Modules:
  0.0 599.3 jit_solution(5333548283131299087)
XLA Ops:
  14.2 6.6 %all-to-all-start.5 = ((f32[128,16,4]{0,2,1:T(4,128)}), f32[128,16,4]{0,2,1:T(4,128)S(1)}, u32[]{:S(2)}, u32[]{:S(2)}) async-start(f32[128,16,4]{0,2,1:T(4,128)} %bitcast.29), calls=%async_computation.5 | async-start | bytes 65536 | tf_op jit(solution)/shard_map/all_to_all | solution.py:44
  43.1 25.9 %all-to-all-done.3 = bf16[128,16,512]{0,2,1:T(8,128)(2,1)} async-done(((bf16[128,16,512]{0,2,1:T(8,128)(2,1)}), bf16[128,16,512]{0,2,1:T(8,128)(2,1)}, u32[]{:S(2)}, u32[]{:S(2)}) %all-to-all-start.3) | async-done | bytes 2097184 | tf_op jit(solution)/shard_map/all_to_all | solution.py:40
  74.2 27.4 %all-to-all-done = bf16[128,16,512]{0,2,1:T(8,128)(2,1)} async-done(((bf16[128,16,512]{0,2,1:T(8,128)(2,1)}), bf16[128,16,512]{0,2,1:T(8,128)(2,1)}, u32[]{:S(2)}, u32[]{:S(2)}) %all-to-all-start) | async-done | bytes 2097184 | tf_op jit(solution)/shard_map/all_to_all | solution.py:41
  109.8 55.2 %all-to-all-done.1 = bf16[1024,16,128]{2,0,1:T(8,128)(2,1)} async-done(((bf16[1024,16,128]{2,0,1:T(8,128)(2,1)}), bf16[1024,16,128]{2,0,1:T(8,128)(2,1)}, u32[]{:S(2)}, u32[]{:S(2)}) %all-to-all-start.1) | async-done | bytes 4194336 | tf_op jit(solution)/shard_map/all_to_all | solution.py:57
  172.5 56.1 %all-to-all-done.4 = bf16[1024,16,128]{2,0,1:T(8,128)(2,1)} async-done(((bf16[1024,16,128]{2,0,1:T(8,128)(2,1)}), bf16[1024,16,128]{2,0,1:T(8,128)(2,1)}, u32[]{:S(2)}, u32[]{:S(2)}) %all-to-all-start.4) | async-done | bytes 4194336 | tf_op jit(solution)/shard_map/all_to_all | solution.py:58
  228.5 289.7 %while.10 = (s32[]{:T(128)}, bf16[16,128,4,128]{1,3,2,0:T(8,128)(2,1)}, bf16[16,128,4,128]{1,3,2,0:T(8,128)(2,1)}, s32[16,32]{1,0:T(8,128)S(1)}, bf16[128,128,12...) while((s32[]{:T(128)}, ...), condition=%wide.region_2.3_spmd, body=%wide.region_1.2_spmd.sunk | while | flops 1623262336 | bytes 25053420 | solution.py:91
  239.9 5.9 fusion.36
  258.0 5.9 fusion.36
  276.1 5.9 fusion.36
  294.2 5.9 fusion.36
  312.3 5.9 fusion.36
  330.4 5.9 fusion.36
  348.5 5.9 fusion.36
  366.6 5.9 fusion.36
  384.7 5.9 fusion.36
  402.8 5.9 fusion.36
  420.9 5.9 fusion.36
  439.1 5.9 fusion.36
  457.2 5.9 fusion.36
  475.3 5.9 fusion.36
  493.4 5.9 fusion.36
  511.5 5.9 fusion.36
  518.2 29.3 %all_to_all.107 = bf16[16,128,512]{1,2,0:T(8,128)(2,1)S(1)} all-to-all(bf16[16,128,512]{1,2,0:T(8,128)(2,1)} %bitcast.120), channel_id=1, replica_groups=mesh['section'=8,'seq'=16] {'seq'}, dimensions={0} | all-to-all | bytes 4194304 | tf_op jit(solution)/shard_map/all_to_all | solution.py:92
  550.6 47.4 %collective-permute-done = bf16[128,8192]{1,0:T(8,128)(2,1)S(1)} collective-permute-done((bf16[128,8192]{1,0:T(8,128)(2,1)}, bf16[128,8192]{1,0:T(8,128)(2,1)S(1)}, u32[]{:S(2)}, u32[]{:S(2)}) %collective-permute-start) | collective-permute-done | bytes 2097184 | tf_op jit(solution)/shard_map/ppermute | solution.py:12
  (182 shorter events, 255.7 us)
Async XLA Ops:
  0.0 172.5 %copy-start = (s32[1,8,16,32]{3,2,1,0:T(8,128)S(1)}, s32[1,8,16,32]{3,2,1,0:T(8,128)}, u32[]{:S(2)}) copy-start(s32[1,8,16,32]{3,2,1,0:T(8,128)} %param.17) | copy-start | bytes 49156
  2.0 2.7 copy-start.4
  5.2 3.2 copy-start.9
  8.4 3.8 copy-start.2
  12.2 8.5 %copy-start.3 = (bf16[1,128,8192]{2,1,0:T(8,128)(2,1)S(1)}, bf16[1,128,8192]{2,1,0:T(8,128)(2,1)}, u32[]{:S(2)}) copy-start(bf16[1,128,8192]{2,1,0:T(8,128)(2,1)} %param.10) | copy-start | bytes 6291460
  13.4 10.4 %copy-start.8 = (bf16[1,128,64]{1,2,0:T(8,128)(2,1)S(1)}, bf16[1,128,64]{1,2,0:T(8,128)(2,1)}, u32[]{:S(2)}) copy-start(bf16[1,128,64]{1,2,0:T(8,128)(2,1)} %param.13) | copy-start | bytes 49156
  14.2 11.3 %all-to-all-start.5 = ((f32[128,16,4]{0,2,1:T(4,128)}), f32[128,16,4]{0,2,1:T(4,128)S(1)}, u32[]{:S(2)}, u32[]{:S(2)}) async-start(f32[128,16,4]{0,2,1:T(4,128)} %bitcast.29), calls=%async_computation.5 | async-start | bytes 65536 | tf_op jit(solution)/shard_map/all_to_all | solution.py:44
  25.5 9.6 %all-to-all-start.2 = ((f32[128,16,4]{0,2,1:T(4,128)}), f32[128,16,4]{0,2,1:T(4,128)S(1)}, u32[]{:S(2)}, u32[]{:S(2)}) async-start(f32[128,16,4]{0,2,1:T(4,128)} %convert.4), calls=%async_computation.2 | async-start | bytes 65536 | tf_op jit(solution)/shard_map/all_to_all | solution.py:45
  30.2 10.4 %copy-start.5 = (bf16[1,128,8192]{2,1,0:T(8,128)(2,1)S(1)}, bf16[1,128,8192]{2,1,0:T(8,128)(2,1)}, u32[]{:S(2)}) copy-start(bf16[1,128,8192]{2,1,0:T(8,128)(2,1)} %param.11) | copy-start | bytes 6291460
  35.0 33.9 %all-to-all-start.3 = ((bf16[128,16,512]{0,2,1:T(8,128)(2,1)}), bf16[128,16,512]{0,2,1:T(8,128)(2,1)}, u32[]{:S(2)}, u32[]{:S(2)}) async-start(bf16[128,16,512]{0,2,1:T(8,128)(2,1)} %multiply_convert_fusion.1), calls=%async_computation.3 | async-start | bytes 4194304 | tf_op jit(solution)/shard_map/all_to_all | solution.py:40
  43.1 30.2 %copy-start.6 = (bf16[1,1024,1024]{2,1,0:T(8,128)(2,1)S(1)}, bf16[1,1024,1024]{2,1,0:T(8,128)(2,1)}, u32[]{:S(2)}) copy-start(bf16[1,1024,1024]{2,1,0:T(8,128)(2,1)} %param.15) | copy-start | bytes 6291460
  69.0 32.6 %all-to-all-start = ((bf16[128,16,512]{0,2,1:T(8,128)(2,1)}), bf16[128,16,512]{0,2,1:T(8,128)(2,1)}, u32[]{:S(2)}, u32[]{:S(2)}) async-start(bf16[128,16,512]{0,2,1:T(8,128)(2,1)} %bitcast.11), calls=%async_computation | async-start | bytes 4194304 | tf_op jit(solution)/shard_map/all_to_all | solution.py:41
  104.4 4.6 copy-start.7
  104.4 60.7 %all-to-all-start.1 = ((bf16[1024,16,128]{2,0,1:T(8,128)(2,1)}), bf16[1024,16,128]{2,0,1:T(8,128)(2,1)}, u32[]{:S(2)}, u32[]{:S(2)}) async-start(bf16[1024,16,128]{2,0,1:T(8,128)(2,1)} %bitcast.114), calls=%async_computation.1 | async-start | bytes 8388608 | tf_op jit(solution)/shard_map/all_to_all | solution.py:57
  167.8 60.7 %all-to-all-start.4 = ((bf16[1024,16,128]{2,0,1:T(8,128)(2,1)}), bf16[1024,16,128]{2,0,1:T(8,128)(2,1)}, u32[]{:S(2)}, u32[]{:S(2)}) async-start(bf16[1024,16,128]{2,0,1:T(8,128)(2,1)} %bitcast.112), calls=%async_computation.4 | async-start | bytes 8388608 | tf_op jit(solution)/shard_map/all_to_all | solution.py:58
  547.5 51.8 %copy-start.1 = (s32[1,8,16,32]{3,2,1,0:T(8,128)S(1)}, s32[1,8,16,32]{3,2,1,0:T(8,128)}, u32[]{:S(2)}) copy-start(s32[1,8,16,32]{3,2,1,0:T(8,128)} %param.17) | copy-start | bytes 49156
  550.4 47.6 %collective-permute-start = (bf16[128,8192]{1,0:T(8,128)(2,1)}, bf16[128,8192]{1,0:T(8,128)(2,1)S(1)}, u32[]{:S(2)}, u32[]{:S(2)}) collective-permute-start(bf16[128,8192]{1,0:T(8,128)(2,1)} %copy.32), channel_id=1, source_target_pairs={{0,112},{16,0},{32,16},{48,32},{64,48},{80,64},{96,80},{112,96},{1... | collective-permute-start | bytes 6291464 | tf_op jit(solution)/shard_map/ppermute | solution.py:12
where the time goes:
time: 606 us; the launch traced here: 599 us
  waiting for transfers between devices  214 us (35%)
  matrix products  182 us (30%)
  local copies, waits for them, and re-layouts  131 us (22%)
  starting transfers between devices  30.7 us (5%)
  blocking collectives  29.3 us (5%)
  other arithmetic  12.3 us (2%)
    dot_general x16, matrix products, one_block(): jnp.einsum('qhk,kd->qhd', grad_scores, tile_keys, preferred_element_type=...  95.1 us
    dot_general x16, matrix products, one_block(): jnp.einsum('qhd,kd->qhk', query_tile, tile_keys, preferred_element_type=j...  86.8 us
    all_to_all x1, waiting for transfers between devices, shards(): lax.all_to_all(values_repeat, 'seq', split_axis=1, concat_axis=0, tiled=T...  56.1 us
    all_to_all x1, waiting for transfers between devices, shards(): lax.all_to_all(keys_repeat, 'seq', split_axis=1, concat_axis=0, tiled=True)  55.2 us
    ppermute x1, waiting for transfers between devices, passed_along(): return lax.ppermute(value, axis, pairs)  47.4 us
    gather x16, local copies, waits for them, and re-layouts, one_block(): tile_keys = key_blocks[picks].reshape(-1, head_dim)  47 us
    gather x16, local copies, waits for them, and re-layouts, one_block(): tile_values = value_blocks[picks].reshape(-1, head_dim)  46.9 us
    all_to_all x1, blocking collectives, shards(): lax.all_to_all(grads, 'seq', split_axis=0, concat_axis=1, tiled=True)  29.3 us
  transfers between devices with their start and end apart: 7, of which 7 were waited for; matrix products, arithmetic and copies ran while one was open for 2% of the time, Pallas kernels for 0%

commit v1 on v0

v1 whole, which is shorter than its diff:
```python
import functools

import jax
import jax.numpy as jnp
from jax import lax
from jax.experimental import pallas as pl
from jax.experimental.pallas import tpu as pltpu
from jax.sharding import PartitionSpec as P

BLOCK = 128
PICKS_A_TILE = 16
LOG2E = 1.4426950408889634
MESH = pl.DeviceIdType.MESH
CONTRACT_LAST = (((1,), (1,)), ((), ()))
CHIP_STEPS = ((1, 0), (0, 1), (0, 3), (1, 1), (0, 2), (1, 3), (1, 2))


def step_offsets(step):
    core = step % 2
    pair = step // 2
    turn = pair // 2
    return pair % 2, turn + (turn // 2) * (1 - 2 * (turn % 2)), core


def kernel(
    sections, members, heads_here, head_dim, picks_count,
    grad_ref, query_ref, out_in_ref, total_ref, gate_ref, key_ref, value_ref, picks_ref,
    result_ref,
    keys, values, head_query, head_grad, row_pack, row_send, gates, done, own_grad, own_out,
    key_send, key_recv, relay_send, relay_recv, token_send, token_recv, out_send, out_recv, local_sem,
):
    section = lax.axis_index("section")
    me = lax.axis_index("seq")
    chips = members // 2
    ring = chips // 2
    core = me % 2
    chip = me // 2
    high = chip // ring
    low = chip % ring
    width = heads_here * head_dim
    blocks_dev = key_ref.shape[0]
    behind = (section + sections - 1) % sections
    ahead = (section + 1) % sections

    def chip_at(dz, dy):
        return ((high + dz) % 2) * ring + (low + dy) % ring

    def member_at(dz, dy, dc):
        return chip_at(dz, dy) * 2 + (core + dc) % 2

    barrier = pltpu.get_barrier_semaphore()

    def greet(i, carry):
        pl.semaphore_signal(barrier, inc=1, device_id=(section, (me + i) % members), device_id_type=MESH)
        return carry

    def greet_sections(i, carry):
        pl.semaphore_signal(barrier, inc=1, device_id=(behind, i), device_id_type=MESH)
        pl.semaphore_signal(barrier, inc=1, device_id=(ahead, i), device_id_type=MESH)
        return carry

    lax.fori_loop(1, members, greet, 0)
    lax.fori_loop(0, members, greet_sections, 0)

    own_copies = [
        pltpu.make_async_copy(grad_ref, own_grad, local_sem.at[0]),
        pltpu.make_async_copy(out_in_ref, own_out, local_sem.at[1]),
    ]
    for copy in own_copies:
        copy.start()
    pl.semaphore_wait(barrier, members - 1 + 2 * members)

    def columns(index, size):
        return pl.ds(pl.multiple_of(index * size, size), size)

    own_rows = pl.ds(me * blocks_dev, blocks_dev)

    sent = []
    for n, (dz, dy) in enumerate(CHIP_STEPS):
        target = chip_at(dz, dy)
        for a, (source, held) in enumerate(((key_ref, keys), (value_ref, values))):
            copy = pltpu.make_async_remote_copy(
                src_ref=source.at[:, :, columns(target, head_dim)],
                dst_ref=held.at[own_rows],
                send_sem=key_send.at[n, a],
                recv_sem=key_recv.at[n, a],
                device_id=(section, target * 2 + core),
                device_id_type=MESH,
            )
            copy.start()
            sent.append(copy)
    partner = (section, chip * 2 + 1 - core)
    relayed, here = [], []
    for a, (source, held) in enumerate(((key_ref, keys), (value_ref, values))):
        mine = source.at[:, :, columns(chip, head_dim)]
        copy = pltpu.make_async_remote_copy(
            src_ref=mine, dst_ref=held.at[own_rows],
            send_sem=relay_send.at[len(CHIP_STEPS), a], recv_sem=relay_recv.at[len(CHIP_STEPS), a],
            device_id=partner, device_id_type=MESH,
        )
        copy.start()
        relayed.append(copy)
        copy = pltpu.make_async_copy(mine, held.at[own_rows], local_sem.at[2 + a])
        copy.start()
        here.append(copy)

    def token_copy(step, a):
        dz, dy, dc = step_offsets(step)
        target = member_at(2 - dz, ring - dy, dc)
        source, held = ((query_ref, head_query), (grad_ref, head_grad))[a]
        return pltpu.make_async_remote_copy(
            src_ref=source.at[:, columns(target, width)],
            dst_ref=held.at[me],
            send_sem=token_send.at[step, a],
            recv_sem=token_recv.at[step, a],
            device_id=(section, target),
            device_id_type=MESH,
        )

    def row_copy(step):
        dz, dy, dc = step_offsets(step)
        target = member_at(2 - dz, ring - dy, dc)
        return pltpu.make_async_remote_copy(
            src_ref=row_send.at[target],
            dst_ref=row_pack.at[me],
            send_sem=token_send.at[step, 2],
            recv_sem=token_recv.at[step, 2],
            device_id=(section, target),
            device_id_type=MESH,
        )

    for step in range(1, members):
        for a in range(2):
            token_copy(step, a).start()
    for a, (source, held) in enumerate(((query_ref, head_query), (grad_ref, head_grad))):
        copy = pltpu.make_async_copy(source.at[:, columns(me, width)], held.at[me], local_sem.at[4 + a])
        copy.start()
        here.append(copy)

    gate_row = 1.0 / (1.0 + jnp.exp(-gate_ref[...]))
    lanes = lax.broadcasted_iota(jnp.int32, gate_row.shape, 1)
    for h in range(heads_here):
        mine = jnp.sum(jnp.where(lanes == me * heads_here + h, gate_row, 0.0), axis=1, keepdims=True)
        gates[h : h + 1, :] = jnp.broadcast_to(mine, (1, head_dim))
    for copy in own_copies:
        copy.wait()
    tokens = own_grad.shape[0]
    log_total = jnp.log2(total_ref[...].astype(jnp.float32)) + 0.5 * 7.0
    lane = lax.broadcasted_iota(jnp.int32, (tokens, 128), 1)
    packed = jnp.zeros((tokens, 128), jnp.float32)
    for h in range(members * heads_here):
        cut = slice(h * head_dim, (h + 1) * head_dim)
        gated = (own_grad[:, cut].astype(jnp.float32) * gate_row[:, h : h + 1]).astype(jnp.bfloat16)
        delta = jnp.sum(gated.astype(jnp.float32) * own_out[:, cut].astype(jnp.float32), axis=1, keepdims=True)
        at = (h // heads_here) * 2 * heads_here + h % heads_here
        packed = jnp.where(lane == at, delta, packed)
        packed = jnp.where(lane == at + heads_here, log_total[:, h : h + 1], packed)
    row_send[...] = packed.T.reshape(row_send.shape)
    row_pack[me] = row_send[me]

    for n, (dz, dy) in enumerate(CHIP_STEPS):
        origin = chip_at(2 - dz, ring - dy) * 2 + core
        rows = pl.ds(origin * blocks_dev, blocks_dev)
        for a, held in enumerate((keys, values)):
            sent[2 * n + a].wait_recv()
            copy = pltpu.make_async_remote_copy(
                src_ref=held.at[rows], dst_ref=held.at[rows],
                send_sem=relay_send.at[n, a], recv_sem=relay_recv.at[n, a],
                device_id=partner, device_id_type=MESH,
            )
            copy.start()
            relayed.append(copy)
    for step in range(1, members):
        row_copy(step).start()
    for copy in relayed:
        copy.wait_recv()
    for copy in here:
        copy.wait()

    scale = LOG2E * head_dim ** -0.5

    def result_copy(step):
        dz, dy, dc = step_offsets(step)
        block = member_at(dz, dy, dc)
        return pltpu.make_async_remote_copy(
            src_ref=done.at[block],
            dst_ref=result_ref.at[:, columns(me, width)],
            send_sem=out_send.at[block],
            recv_sem=out_recv.at[me],
            device_id=(behind, block),
            device_id_type=MESH,
        )

    def one_block(step, carry):
        dz, dy, dc = step_offsets(step)
        block = member_at(dz, dy, dc)

        @pl.when(step > 0)
        def _():
            result_copy(step - 1).start()
            for a in range(2):
                token_copy(step, a).wait_recv()
            row_copy(step).wait_recv()

        query_all, grad_all = head_query[block], head_grad[block]
        cuts = [slice(h * head_dim, (h + 1) * head_dim) for h in range(heads_here)]
        query = jnp.concatenate([query_all[:, cut] for cut in cuts], 0)
        grad = jnp.concatenate(
            [
                (grad_all[:, cut].astype(jnp.float32) * gates[h : h + 1, :]).astype(jnp.bfloat16)
                for h, cut in enumerate(cuts)
            ],
            0,
        )
        per_row = row_pack[block].T
        delta = jnp.concatenate([per_row[:, h : h + 1] for h in range(heads_here)], 0)
        log_total = jnp.concatenate([per_row[:, heads_here + h : heads_here + h + 1] for h in range(heads_here)], 0)

        def tile(t, total):
            picked = [picks_ref[chip, block, t * PICKS_A_TILE + i] for i in range(PICKS_A_TILE)]
            tile_keys = jnp.concatenate([keys[pick] for pick in picked], 0)
            tile_values = jnp.concatenate([values[pick] for pick in picked], 0)
            scores = lax.dot_general(query, tile_keys, CONTRACT_LAST, preferred_element_type=jnp.float32)
            grad_probs = lax.dot_general(grad, tile_values, CONTRACT_LAST, preferred_element_type=jnp.float32)
            probs = jnp.exp2(scores * scale - log_total)
            grad_scores = (probs * (grad_probs - delta)).astype(jnp.bfloat16)
            return total + jnp.dot(grad_scores, tile_keys, preferred_element_type=jnp.float32)

        total = lax.fori_loop(
            0, picks_count // PICKS_A_TILE, tile, jnp.zeros((heads_here * tokens, head_dim), jnp.float32)
        )
        for h, cut in enumerate(cuts):
            done[block, :, cut] = total[h * tokens : (h + 1) * tokens].astype(jnp.bfloat16)
        return carry

    lax.fori_loop(0, members, one_block, 0)
    result_copy(members - 1).start()

    for copy in sent:
        copy.wait_send()
    for copy in relayed:
        copy.wait_send()

    def drain(step, carry):
        for a in range(2):
            token_copy(step, a).wait_send()
        row_copy(step).wait_send()
        return carry

    lax.fori_loop(1, members, drain, 0)

    def settle(i, carry):
        copy = pltpu.make_async_remote_copy(
            src_ref=done.at[i],
            dst_ref=result_ref.at[:, columns(i, width)],
            send_sem=out_send.at[i],
            recv_sem=out_recv.at[i],
            device_id=(behind, i),
            device_id_type=MESH,
        )
        copy.wait_send()
        copy.wait_recv()
        return carry

    lax.fori_loop(0, members, settle, 0)


def shards(grad_out, queries, mem_out, row_total, gate_logit, mem_keys, mem_values, retrieved):
    members = lax.axis_size("seq")
    sections = lax.axis_size("section")
    tokens, full_width = grad_out.shape[1:]
    head_count = gate_logit.shape[1]
    head_dim = full_width // head_count
    heads_here = head_count // members
    width = heads_here * head_dim
    mem_dev = mem_keys.shape[1]
    blocks_dev = mem_dev // BLOCK
    mem_blocks = blocks_dev * members
    any_space = pl.BlockSpec(memory_space=pl.ANY)
    vmem = pl.BlockSpec(memory_space=pltpu.VMEM)
    dma = pltpu.SemaphoreType.DMA
    steps = len(CHIP_STEPS)
    result = pl.pallas_call(
        functools.partial(kernel, sections, members, heads_here, head_dim, retrieved.shape[3]),
        out_shape=jax.ShapeDtypeStruct((tokens, full_width), jnp.bfloat16),
        in_specs=[any_space, any_space, any_space, vmem, vmem, any_space, any_space,
                  pl.BlockSpec(memory_space=pltpu.SMEM)],
        out_specs=any_space,
        scratch_shapes=[
            pltpu.VMEM((mem_blocks, BLOCK, head_dim), jnp.bfloat16),
            pltpu.VMEM((mem_blocks, BLOCK, head_dim), jnp.bfloat16),
            pltpu.VMEM((members, tokens, width), jnp.bfloat16),
            pltpu.VMEM((members, tokens, width), jnp.bfloat16),
            pltpu.VMEM((members, 2 * heads_here, tokens), jnp.float32),
            pltpu.VMEM((members, 2 * heads_here, tokens), jnp.float32),
            pltpu.VMEM((8, head_dim), jnp.float32),
            pltpu.VMEM((members, tokens, width), jnp.bfloat16),
            pltpu.VMEM((tokens, full_width), jnp.bfloat16),
            pltpu.VMEM((tokens, full_width), jnp.bfloat16),
            dma((steps, 2)),
            dma((steps, 2)),
            dma((steps + 1, 2)),
            dma((steps + 1, 2)),
            dma((members, 3)),
            dma((members, 3)),
            dma((members,)),
            dma((members,)),
            dma((6,)),
        ],
        compiler_params=pltpu.CompilerParams(
            collective_id=0, has_side_effects=True, vmem_limit_bytes=60 * 1024 * 1024
        ),
        name="relay_attention_backward",
    )(
        grad_out[0],
        queries[0],
        mem_out[0],
        row_total[0],
        gate_logit,
        mem_keys[0].reshape(blocks_dev, BLOCK, mem_keys.shape[2]),
        mem_values[0].reshape(blocks_dev, BLOCK, mem_values.shape[2]),
        retrieved[0],
    )
    return result[None]


def solution(mesh):
    return jax.shard_map(
        shards,
        mesh=mesh,
        in_specs=(
            P("section", "seq", None),
            P("section", "seq", None),
            P("section", "seq", None),
            P("section", "seq", None),
            P("section", None),
            P("section", "seq", None),
            P("section", "seq", None),
            P("section", None, None, None),
        ),
        out_specs=P("section", "seq", None),
        check_vma=False,
    )
```

time: 606 us -> 185 us (0.31)
  waiting for transfers between devices: 214 us -> 0 us
  matrix products: 182 us -> 0 us
  Pallas kernels: 0 us -> 180 us
  local copies, waits for them, and re-layouts: 131 us -> 4.53 us
  starting transfers between devices: 30.7 us -> 0 us
  blocking collectives: 29.3 us -> 0 us
  other arithmetic: 12.3 us -> 0 us
    dot_general x32 -> x0, matrix products: 182 us -> none  [the longest x16 95.1 us: one_block(): jnp.einsum('qhk,kd->qhd', grad_scores, tile_keys, preferred_element_type=...]
    pallas_call x0 -> x1, Pallas kernels: none -> 180 us  [shards(): pl.pallas_call(functools.partial(kernel, sections, members, heads_here, h...]
    all_to_all x6 -> x0, waiting for transfers between devices: 166 us -> none  [the longest x1 56.1 us: shards(): lax.all_to_all(values_repeat, 'seq', split_axis=1, concat_axis=0, tiled=T...]
    gather x32 -> x0, local copies, waits for them, and re-layouts: 93.9 us -> none  [the longest x16 47 us: one_block(): tile_keys = key_blocks[picks].reshape(-1, head_dim)]
    ppermute x1 -> x0, waiting for transfers between devices: 47.4 us -> none  [passed_along(): return lax.ppermute(value, axis, pairs)]
    all_to_all x6 -> x0, starting transfers between devices: 30.5 us -> none  [the longest x1 6.57 us: shards(): lax.all_to_all(token_delta, 'seq', split_axis=1, concat_axis=0, tiled=True)]
    all_to_all x1 -> x0, blocking collectives: 29.3 us -> none  [shards(): lax.all_to_all(grads, 'seq', split_axis=0, concat_axis=1, tiled=True)]
    dynamic_update_slice x32 -> x0, local copies, waits for them, and re-layouts: 12.9 us -> none  [shards(): lax.map(one_block, blocks_in).reshape(tokens, local_heads * head_dim)]
  transfers between devices with their start and end apart: 7 -> 0, of which waited for: 7 -> 0; matrix products, arithmetic and copies ran while one was open for 2% -> 0% of each run, Pallas kernels for 0% -> 0%
where the time goes in v1:
time: 185 us; the launch traced here: 184 us
  Pallas kernels  180 us (97%)
  local copies, waits for them, and re-layouts  4.53 us (2%)
    pallas_call x1, Pallas kernels, shards(): pl.pallas_call(functools.partial(kernel, sections, members, heads_here, h...  180 us
    unnamed x2, local copies, waits for them, and re-layouts  4.53 us

profile of v1, /device:TPU:13, one launch (start us, length us, event | category | flops | bytes accessed | tf_op | source)
XLA Modules:
  0.0 184.2 jit_solution(5511955348097909986)
XLA Ops:
  0.0 1.4 copy.9
  1.4 179.7 %relay_attention_backward.1 = bf16[128,8192]{1,0:T(8,128)(2,1)} custom-call(bf16[128,8192]{1,0:T(8,128)(2,1)} %bitcast.9, bf16[128,8192]{1,0:T(8,128)(2,1)} %bitcast.10, bf16[128,8192]{1,0:T(8,128)(2,1)} %bitcast.11, bf16[128,64]{1,0:T(8,128)(2,1)} %bitcast.14, f32[1,64]{1,0:T(1,128)} %gate_ref.1, bf16[8,128,1024]{2,1,0:T(8,128)(2,1)} %bitcast.12, ...), custom_call_target="tpu_custom_call" | custom-call | tf_op jit(solution)/shard_map/relay_attention_backward/pallas_call | solution.py:283
  181.1 3.1 %copy.11 = bf16[1,128,8192]{2,1,0:T(8,128)(2,1)} copy(bf16[1,128,8192]{2,1,0:T(8,128)(2,1)} %bitcast.8) | data formatting | bytes 4194304

commit v2 on v1

v2 whole, which is shorter than its diff:
```python
import functools

import jax
import jax.numpy as jnp
from jax import lax
from jax.experimental import pallas as pl
from jax.experimental.pallas import tpu as pltpu
from jax.sharding import PartitionSpec as P

BLOCK = 128
PICKS_A_TILE = 16
AHEAD = 4
FORWARD_FROM = 10
SHIFT = 1
LOG2E = 1.4426950408889634
MESH = pl.DeviceIdType.MESH
CONTRACT_LAST = (((1,), (1,)), ((), ()))
CHIP_STEPS = ((1, 0), (0, 1), (0, 3), (1, 1), (0, 2), (1, 3), (1, 2))


def step_offsets(step, core):
    away = (step + 12) // 14
    turn = (step + 5 + SHIFT * core) % 7
    pair = turn // 2 + turn % 2
    along = pair + (pair // 2) * (1 - 2 * (pair % 2))
    return away * (1 - turn % 2), away * along, (1 - away) * step + away * ((step + 5) // 7 - 1)


def kernel(
    sections, members, heads_here, head_dim, picks_count,
    grad_ref, query_ref, out_in_ref, total_ref, gate_ref, key_ref, value_ref, picks_ref,
    result_ref,
    memory, head_rows, memory_send, rows_send, row_pack, row_send, gates, done, passed, own_grad, own_out,
    key_send, key_recv, relay_send, relay_recv, token_send, token_recv, pass_send, pass_recv, out_send, out_recv, local_sem, stage_sem,
):
    section = lax.axis_index("section")
    me = lax.axis_index("seq")
    chips = members // 2
    ring = chips // 2
    core = me % 2
    chip = me // 2
    high = chip // ring
    low = chip % ring
    width = heads_here * head_dim
    blocks_dev = key_ref.shape[0]
    behind = (section + sections - 1) % sections
    ahead = (section + 1) % sections
    half = sections // 2
    turned_out = 1 - (section % half + half - 1) // half
    turned_in = 1 - (ahead % half + half - 1) // half
    relay_to = (((high + turned_out) % 2) * ring + low) * 2 + core
    source_high = (high + turned_in) % 2
    source = (source_high * ring + low) * 2 + core

    def chip_at(dz, dy):
        return ((high + dz) % 2) * ring + (low + dy) % ring

    def member_at(dz, dy, dc):
        return chip_at(dz, dy) * 2 + (core + dc) % 2

    barrier = pltpu.get_barrier_semaphore()

    def greet(i, carry):
        pl.semaphore_signal(barrier, inc=1, device_id=(section, (me + i) % members), device_id_type=MESH)
        return carry

    lax.fori_loop(1, members, greet, 0)
    pl.semaphore_signal(barrier, inc=1, device_id=(ahead, source), device_id_type=MESH)

    def columns(index, size):
        return pl.ds(pl.multiple_of(index * size, size), size)

    own_rows = pl.ds(me * blocks_dev, blocks_dev)

    def gather_memory(target, a, slot):
        return pltpu.make_async_copy(
            (key_ref, value_ref)[a].at[:, :, columns(target, head_dim)], memory_send.at[target, a], slot
        )

    def gather_rows(target, a, slot):
        return pltpu.make_async_copy(
            (query_ref, grad_ref)[a].at[:, columns(target, width)], rows_send.at[target, a], slot
        )

    for target in range(chips):
        for a in range(2):
            gather_memory(target, a, stage_sem.at[target, a]).start()
    own_copies = [
        pltpu.make_async_copy(grad_ref, own_grad, local_sem.at[0]),
        pltpu.make_async_copy(out_in_ref, own_out, local_sem.at[1]),
    ]
    for copy in own_copies:
        copy.start()
    for target in range(members):
        for a in range(2):
            gather_rows(target, a, stage_sem.at[chips + target, a]).start()
    pl.semaphore_wait(barrier, members)
    for target in range(chips):
        for a in range(2):
            gather_memory(target, a, stage_sem.at[target, a]).wait()

    sent = []
    for n, (dz, dy) in enumerate(CHIP_STEPS):
        target = chip_at(dz, dy)
        copy = pltpu.make_async_remote_copy(
            src_ref=memory_send.at[target],
            dst_ref=memory.at[:, own_rows],
            send_sem=key_send.at[n],
            recv_sem=key_recv.at[n],
            device_id=(section, target * 2 + core),
            device_id_type=MESH,
        )
        copy.start()
        sent.append(copy)
    partner = (section, chip * 2 + 1 - core)
    here = [
        pltpu.make_async_copy(memory_send.at[chip], memory.at[:, own_rows], local_sem.at[2]),
        pltpu.make_async_copy(rows_send.at[me], head_rows.at[me], local_sem.at[3]),
    ]
    copy = pltpu.make_async_remote_copy(
        src_ref=memory_send.at[chip], dst_ref=memory.at[:, own_rows],
        send_sem=relay_send.at[len(CHIP_STEPS)], recv_sem=relay_recv.at[len(CHIP_STEPS)],
        device_id=partner, device_id_type=MESH,
    )
    copy.start()
    relayed = [copy]

    def token_target(step):
        dc = step_offsets(step, core)[2]
        dz, dy, dc = step_offsets(step, (core + dc) % 2)
        return member_at(2 - dz, ring - dy, dc)

    def token_copy(step):
        target = token_target(step)
        return pltpu.make_async_remote_copy(
            src_ref=rows_send.at[target],
            dst_ref=head_rows.at[me],
            send_sem=token_send.at[step, 0],
            recv_sem=token_recv.at[step, 0],
            device_id=(section, target),
            device_id_type=MESH,
        )

    def row_copy(step):
        target = token_target(step)
        return pltpu.make_async_remote_copy(
            src_ref=row_send.at[target],
            dst_ref=row_pack.at[me],
            send_sem=token_send.at[step, 1],
            recv_sem=token_recv.at[step, 1],
            device_id=(section, target),
            device_id_type=MESH,
        )

    for target in range(members):
        for a in range(2):
            gather_rows(target, a, stage_sem.at[chips + target, a]).wait()
    token_copy(1).start()
    for copy in here:
        copy.start()

    gate_row = 1.0 / (1.0 + jnp.exp(-gate_ref[...]))
    lanes = lax.broadcasted_iota(jnp.int32, gate_row.shape, 1)
    for h in range(heads_here):
        mine = jnp.sum(jnp.where(lanes == me * heads_here + h, gate_row, 0.0), axis=1, keepdims=True)
        gates[h : h + 1, :] = jnp.broadcast_to(mine, (1, head_dim))
    for copy in own_copies:
        copy.wait()
    tokens = own_grad.shape[0]
    log_total = jnp.log2(total_ref[...].astype(jnp.float32)) + 0.5 * 7.0
    lane = lax.broadcasted_iota(jnp.int32, (tokens, tokens), 1)
    packed = jnp.zeros((tokens, tokens), jnp.float32)
    for h in range(members * heads_here):
        cut = slice(h * head_dim, (h + 1) * head_dim)
        gated = (own_grad[:, cut].astype(jnp.float32) * gate_row[:, h : h + 1]).astype(jnp.bfloat16)
        delta = jnp.sum(gated.astype(jnp.float32) * own_out[:, cut].astype(jnp.float32), axis=1, keepdims=True)
        packed = jnp.where(lane == h, delta, packed)
    packed = packed.T
    for i in range(members):
        cut = slice(i * heads_here, (i + 1) * heads_here)
        row_send[i] = jnp.concatenate([packed[cut], log_total[cut]], 0)
    row_pack[me] = row_send[me]
    for step in range(1, members):
        row_copy(step).start()
    for step in range(2, AHEAD):
        token_copy(step).start()

    for n, (dz, dy) in enumerate(CHIP_STEPS):
        origin = chip_at(2 - dz, ring - dy) * 2 + core
        rows = pl.ds(origin * blocks_dev, blocks_dev)
        sent[n].wait_recv()
        copy = pltpu.make_async_remote_copy(
            src_ref=memory.at[:, rows], dst_ref=memory.at[:, rows],
            send_sem=relay_send.at[n], recv_sem=relay_recv.at[n],
            device_id=partner, device_id_type=MESH,
        )
        copy.start()
        relayed.append(copy)
    for copy in relayed:
        copy.wait_recv()
    for copy in here:
        copy.wait()

    scale = LOG2E * head_dim ** -0.5

    def pass_copy(step):
        return pltpu.make_async_remote_copy(
            src_ref=done.at[step],
            dst_ref=passed.at[step],
            send_sem=pass_send.at[step],
            recv_sem=pass_recv.at[step],
            device_id=(behind, relay_to),
            device_id_type=MESH,
        )

    def owner_of(step):
        dz, dy, dc = step_offsets(step, core)
        return (((source_high + dz) % 2) * ring + (low + dy) % ring) * 2 + (core + dc) % 2

    def result_copy(step):
        return pltpu.make_async_remote_copy(
            src_ref=passed.at[step],
            dst_ref=result_ref.at[:, columns(source, width)],
            send_sem=out_send.at[step],
            recv_sem=out_recv.at[source],
            device_id=(section, owner_of(step)),
            device_id_type=MESH,
        )

    def result_here(step):
        return pltpu.make_async_copy(passed.at[step], result_ref.at[:, columns(source, width)], local_sem.at[4])

    def forward(step, carry):
        owner = owner_of(step)
        pass_copy(step).wait_recv()

        @pl.when(owner != me)
        def _():
            result_copy(step).start()

        @pl.when(owner == me)
        def _():
            result_here(step).start()

        return carry

    def one_block(step, carry):
        dz, dy, dc = step_offsets(step, core)
        block = member_at(dz, dy, dc)

        @pl.when(step > 0)
        def _():
            pass_copy(step - 1).start()

        @pl.when(step < members - AHEAD)
        def _():
            token_copy(step + AHEAD).start()

        @pl.when(step > 0)
        def _():
            token_copy(step).wait_recv()
            row_copy(step).wait_recv()

        @pl.when(step >= FORWARD_FROM)
        def _():
            first = (step - FORWARD_FROM) * 2
            lax.fori_loop(first, first + 2, forward, 0)

        query_all, grad_all = head_rows[block, 0], head_rows[block, 1]
        cuts = [slice(h * head_dim, (h + 1) * head_dim) for h in range(heads_here)]
        query = jnp.concatenate([query_all[:, cut] for cut in cuts], 0)
        grad = jnp.concatenate(
            [
                (grad_all[:, cut].astype(jnp.float32) * gates[h : h + 1, :]).astype(jnp.bfloat16)
                for h, cut in enumerate(cuts)
            ],
            0,
        )
        per_row = row_pack[block].T
        delta = jnp.concatenate([per_row[:, h : h + 1] for h in range(heads_here)], 0)
        log_total = jnp.concatenate([per_row[:, heads_here + h : heads_here + h + 1] for h in range(heads_here)], 0)

        def tile(t, total):
            picked = [picks_ref[chip, block, t * PICKS_A_TILE + i] for i in range(PICKS_A_TILE)]
            tile_keys = jnp.concatenate([memory[0, pick] for pick in picked], 0)
            tile_values = jnp.concatenate([memory[1, pick] for pick in picked], 0)
            scores = lax.dot_general(query, tile_keys, CONTRACT_LAST, preferred_element_type=jnp.float32)
            grad_probs = lax.dot_general(grad, tile_values, CONTRACT_LAST, preferred_element_type=jnp.float32)
            probs = jnp.exp2(scores * scale - log_total)
            grad_scores = (probs * (grad_probs - delta)).astype(jnp.bfloat16)
            return total + jnp.dot(grad_scores, tile_keys, preferred_element_type=jnp.float32)

        total = lax.fori_loop(
            0, picks_count // PICKS_A_TILE, tile, jnp.zeros((heads_here * tokens, head_dim), jnp.float32)
        )
        for h, cut in enumerate(cuts):
            done[step, :, cut] = total[h * tokens : (h + 1) * tokens].astype(jnp.bfloat16)
        return carry

    lax.fori_loop(0, members, one_block, 0)
    pass_copy(members - 1).start()
    lax.fori_loop((members - FORWARD_FROM) * 2, members, forward, 0)

    for copy in sent:
        copy.wait_send()
    for copy in relayed:
        copy.wait_send()

    def drain(step, carry):
        token_copy(step).wait_send()
        row_copy(step).wait_send()
        return carry

    lax.fori_loop(1, members, drain, 0)

    def settle(step, carry):
        pass_copy(step).wait_send()

        @pl.when(owner_of(step) != me)
        def _():
            result_copy(step).wait_send()

        @pl.when(owner_of(step) == me)
        def _():
            result_here(step).wait()

        @pl.when(step != source)
        def _():
            pltpu.make_async_remote_copy(
                src_ref=passed.at[step],
                dst_ref=result_ref.at[:, columns(step, width)],
                send_sem=out_send.at[step],
                recv_sem=out_recv.at[step],
                device_id=partner,
                device_id_type=MESH,
            ).wait_recv()

        return carry

    lax.fori_loop(0, members, settle, 0)


def shards(grad_out, queries, mem_out, row_total, gate_logit, mem_keys, mem_values, retrieved):
    members = lax.axis_size("seq")
    sections = lax.axis_size("section")
    tokens, full_width = grad_out.shape[1:]
    head_count = gate_logit.shape[1]
    head_dim = full_width // head_count
    heads_here = head_count // members
    width = heads_here * head_dim
    mem_dev = mem_keys.shape[1]
    blocks_dev = mem_dev // BLOCK
    mem_blocks = blocks_dev * members
    any_space = pl.BlockSpec(memory_space=pl.ANY)
    vmem = pl.BlockSpec(memory_space=pltpu.VMEM)
    dma = pltpu.SemaphoreType.DMA
    steps = len(CHIP_STEPS)
    result = pl.pallas_call(
        functools.partial(kernel, sections, members, heads_here, head_dim, retrieved.shape[3]),
        out_shape=jax.ShapeDtypeStruct((tokens, full_width), jnp.bfloat16),
        in_specs=[any_space, any_space, any_space, vmem, vmem, any_space, any_space,
                  pl.BlockSpec(memory_space=pltpu.SMEM)],
        out_specs=any_space,
        scratch_shapes=[
            pltpu.VMEM((2, mem_blocks, BLOCK, head_dim), jnp.bfloat16),
            pltpu.VMEM((members, 2, tokens, width), jnp.bfloat16),
            pltpu.VMEM((members // 2, 2, blocks_dev, BLOCK, head_dim), jnp.bfloat16),
            pltpu.VMEM((members, 2, tokens, width), jnp.bfloat16),
            pltpu.VMEM((members, 2 * heads_here, tokens), jnp.float32),
            pltpu.VMEM((members, 2 * heads_here, tokens), jnp.float32),
            pltpu.VMEM((8, head_dim), jnp.float32),
            pltpu.VMEM((members, tokens, width), jnp.bfloat16),
            pltpu.VMEM((members, tokens, width), jnp.bfloat16),
            pltpu.VMEM((tokens, full_width), jnp.bfloat16),
            pltpu.VMEM((tokens, full_width), jnp.bfloat16),
            dma((steps,)),
            dma((steps,)),
            dma((steps + 1,)),
            dma((steps + 1,)),
            dma((members, 2)),
            dma((members, 2)),
            dma((members,)),
            dma((members,)),
            dma((members,)),
            dma((members,)),
            dma((5,)),
            dma((members // 2 + members, 2)),
        ],
        compiler_params=pltpu.CompilerParams(
            collective_id=0, has_side_effects=True, vmem_limit_bytes=60 * 1024 * 1024
        ),
        name="relay_attention_backward",
    )(
        grad_out[0],
        queries[0],
        mem_out[0],
        row_total[0].T,
        gate_logit,
        mem_keys[0].reshape(blocks_dev, BLOCK, mem_keys.shape[2]),
        mem_values[0].reshape(blocks_dev, BLOCK, mem_values.shape[2]),
        retrieved[0],
    )
    return result[None]


def solution(mesh):
    return jax.shard_map(
        shards,
        mesh=mesh,
        in_specs=(
            P("section", "seq", None),
            P("section", "seq", None),
            P("section", "seq", None),
            P("section", "seq", None),
            P("section", None),
            P("section", "seq", None),
            P("section", "seq", None),
            P("section", None, None, None),
        ),
        out_specs=P("section", "seq", None),
        check_vma=False,
    )
```

time: 185 us -> 147 us (0.79)
  the two profiles are of different devices: /device:TPU:13 before, /device:TPU:25 now
where the time goes in v2:
time: 147 us
  Pallas kernels  144 us (98%)
  local copies, waits for them, and re-layouts  3.1 us (2%)
    pallas_call x1, Pallas kernels, shards(): pl.pallas_call(functools.partial(kernel, sections, members, heads_here, h...  144 us
    unnamed x1, local copies, waits for them, and re-layouts  3.1 us

profile of v2, /device:TPU:25, one launch (start us, length us, event | category | flops | bytes accessed | tf_op | source)
XLA Modules:
  0.0 146.9 jit_solution(12763502509026401528)
XLA Ops:
  0.0 143.8 %relay_attention_backward.1 = bf16[128,8192]{1,0:T(8,128)(2,1)} custom-call(bf16[128,8192]{1,0:T(8,128)(2,1)} %bitcast.11, bf16[128,8192]{1,0:T(8,128)(2,1)} %bitcast.12, bf16[128,8192]{1,0:T(8,128)(2,1)} %bitcast.13, bf16[64,128]{1,0:T(8,128)(2,1)} %bitcast.17, f32[1,64]{1,0:T(1,128)} %gate_ref.1, bf16[8,128,1024]{2,1,0:T(8,128)(2,1)} %bitcast.14, ...), custom_call_target="tpu_custom_call" | custom-call | tf_op jit(solution)/shard_map/relay_attention_backward/pallas_call | solution.py:358
  143.8 3.1 %copy.10 = bf16[1,128,8192]{2,1,0:T(8,128)(2,1)} copy(bf16[1,128,8192]{2,1,0:T(8,128)(2,1)} %bitcast.10) | data formatting | bytes 4194304

commit v3 on v2

--- a/solution.py
+++ b/solution.py
@@ -9,8 +9,8 @@
 
 BLOCK = 128
 PICKS_A_TILE = 16
-AHEAD = 4
-FORWARD_FROM = 10
+AHEAD = 6
+FORWARD_FROM = 9
 SHIFT = 1
 LOG2E = 1.4426950408889634
 MESH = pl.DeviceIdType.MESH

time: 147 us -> 140 us (0.952)
  the two profiles are of different devices: /device:TPU:25 before, /device:TPU:13 now
where the time goes in v3:
time: 140 us; the launch traced here: 139 us
  Pallas kernels  136 us (97%)
  local copies, waits for them, and re-layouts  3.1 us (2%)
    pallas_call x1, Pallas kernels, shards(): pl.pallas_call(functools.partial(kernel, sections, members, heads_here, h...  136 us
    unnamed x1, local copies, waits for them, and re-layouts  3.1 us

profile of v3, /device:TPU:13, one launch (start us, length us, event | category | flops | bytes accessed | tf_op | source)
XLA Modules:
  0.0 139.0 jit_solution(17409149149639939686)
XLA Ops:
  0.0 135.9 %relay_attention_backward.1 = bf16[128,8192]{1,0:T(8,128)(2,1)} custom-call(bf16[128,8192]{1,0:T(8,128)(2,1)} %bitcast.11, bf16[128,8192]{1,0:T(8,128)(2,1)} %bitcast.12, bf16[128,8192]{1,0:T(8,128)(2,1)} %bitcast.13, bf16[64,128]{1,0:T(8,128)(2,1)} %bitcast.17, f32[1,64]{1,0:T(1,128)} %gate_ref.1, bf16[8,128,1024]{2,1,0:T(8,128)(2,1)} %bitcast.14, ...), custom_call_target="tpu_custom_call" | custom-call | tf_op jit(solution)/shard_map/relay_attention_backward/pallas_call | solution.py:358
  135.9 3.1 %copy.10 = bf16[1,128,8192]{2,1,0:T(8,128)(2,1)} copy(bf16[1,128,8192]{2,1,0:T(8,128)(2,1)} %bitcast.10) | data formatting | bytes 4194304
